TPU v7x, 32 devices: a whole 2x2x4 slice. The times are simulated.
32 devices in a mesh: blk: 8 (over z, x), head: 4 (over y, core).
Axes of the slice: x: 2, y: 2, z: 4, core: 2. Of those that a mesh axis runs over, the one named last changes fastest.
Arguments:
- tokens: float32 [4096, 1536], P(('blk', 'head')), may hold values from -6 to 6
- cotangent: float32 [4096, 1536], P(('blk', 'head')), may hold values from -6 to 6
- doc_starts: int32 [4096], P('blk'), may hold values from 0 to 4095, as said below
- routes: int32 [4096, 6], P(('blk', 'head')), may hold values from 0 to 63, as said below
- expert_slots: int32 [4096, 6], P(('blk', 'head')), may hold values from -1 to 15, as said below
- norm_gains: float32 [2, 1536], P(None, ('blk', 'head')), may hold values from 0.25 to 1.75
- qkv_projection_weight: float32 [1536, 2560], P(('blk', 'head')), may hold values from -0.15625 to 0.15625
- w_out: float32 [1536, 1536], P(None, ('blk', 'head')), may hold values from -0.5 to 0.5
- w_router: float32 [1536, 64], P(('blk', 'head')), may hold values from -0.3125 to 0.3125
- w_moe_in: float32 [64, 1536, 1024], P('blk', 'head'), may hold values from -0.15625 to 0.15625
- w_moe_out: float32 [64, 512, 1536], P('blk', None, 'head'), may hold values from -0.5 to 0.5
- w_shared_in: float32 [1536, 2048], P(('blk', 'head')), may hold values from -0.15625 to 0.15625
- w_shared_out: float32 [1024, 1536], P(None, ('blk', 'head')), may hold values from -0.375 to 0.375
- mom_norm_gains: float32 [2, 1536], P(None, ('blk', 'head')), may hold values from -115.2 to 115.2
- momentum_qkv_weight: float32 [1536, 2560], P(('blk', 'head')), may hold values from -76.8 to 76.8
- mom_w_out: float32 [1536, 1536], P(None, ('blk', 'head')), may hold values from -115.2 to 115.2
- mom_w_router: float32 [1536, 64], P(('blk', 'head')), may hold values from -1152 to 1152
- mom_w_moe_in: float32 [64, 1536, 1024], P('blk', 'head'), may hold values from -24 to 24
- mom_w_moe_out: float32 [64, 512, 1536], P('blk', None, 'head'), may hold values from -24 to 24
- mom_w_shared_in: float32 [1536, 2048], P(('blk', 'head')), may hold values from -115.2 to 115.2
- mom_w_shared_out: float32 [1024, 1536], P(None, ('blk', 'head')), may hold values from -192 to 192
- avg_norm_gains: float32 [2, 1536], P(None, ('blk', 'head')), may hold values from 0.25 to 1.75
- averaged_qkv_weight: float32 [1536, 2560], P(('blk', 'head')), may hold values from -0.3125 to 0.3125
- avg_w_out: float32 [1536, 1536], P(None, ('blk', 'head')), may hold values from -0.5 to 0.5
- avg_w_router: float32 [1536, 64], P(('blk', 'head')), may hold values from -0.3125 to 0.3125
- avg_w_moe_in: float32 [64, 1536, 1024], P('blk', 'head'), may hold values from -0.3125 to 0.3125
- avg_w_moe_out: float32 [64, 512, 1536], P('blk', None, 'head'), may hold values from -0.5 to 0.5
- avg_w_shared_in: float32 [1536, 2048], P(('blk', 'head')), may hold values from -0.3125 to 0.3125
- avg_w_shared_out: float32 [1024, 1536], P(None, ('blk', 'head')), may hold values from -0.375 to 0.375
Outputs:
- output: float32 [4096, 1536], P(('blk', 'head'))
- grad_tokens: float32 [4096, 1536], P(('blk', 'head'))
- grad_norm_gains: float32 [2, 1536], P(None, ('blk', 'head'))
- new_norm_gains: float32 [2, 1536], P(None, ('blk', 'head'))
- next_mom_norm_gains: float32 [2, 1536], P(None, ('blk', 'head'))
- next_avg_norm_gains: float32 [2, 1536], P(None, ('blk', 'head'))
- grad_w_qkv: float32 [1536, 2560], P(('blk', 'head'))
- new_w_qkv: float32 [1536, 2560], P(('blk', 'head'))
- next_mom_w_qkv: float32 [1536, 2560], P(('blk', 'head'))
- next_avg_w_qkv: float32 [1536, 2560], P(('blk', 'head'))
- grad_w_out: float32 [1536, 1536], P(None, ('blk', 'head'))
- new_w_out: float32 [1536, 1536], P(None, ('blk', 'head'))
- next_mom_w_out: float32 [1536, 1536], P(None, ('blk', 'head'))
- next_avg_w_out: float32 [1536, 1536], P(None, ('blk', 'head'))
- grad_w_router: float32 [1536, 64], P(('blk', 'head'))
- new_w_router: float32 [1536, 64], P(('blk', 'head'))
- next_mom_w_router: float32 [1536, 64], P(('blk', 'head'))
- next_avg_w_router: float32 [1536, 64], P(('blk', 'head'))
- grad_w_moe_in: float32 [64, 1536, 1024], P('blk', 'head')
- new_w_moe_in: float32 [64, 1536, 1024], P('blk', 'head')
- next_mom_w_moe_in: float32 [64, 1536, 1024], P('blk', 'head')
- next_avg_w_moe_in: float32 [64, 1536, 1024], P('blk', 'head')
- grad_w_moe_out: float32 [64, 512, 1536], P('blk', None, 'head')
- step_w_moe_out: float32 [64, 512, 1536], P('blk', None, 'head')
- next_mom_w_moe_out: float32 [64, 512, 1536], P('blk', None, 'head')
- next_avg_w_moe_out: float32 [64, 512, 1536], P('blk', None, 'head')
- grad_w_shared_in: float32 [1536, 2048], P(('blk', 'head'))
- new_w_shared_in: float32 [1536, 2048], P(('blk', 'head'))
- next_mom_w_shared_in: float32 [1536, 2048], P(('blk', 'head'))
- next_avg_w_shared_in: float32 [1536, 2048], P(('blk', 'head'))
- grad_w_shared_out: float32 [1024, 1536], P(None, ('blk', 'head'))
- new_w_shared_out: float32 [1024, 1536], P(None, ('blk', 'head'))
- next_mom_w_shared_out: float32 [1024, 1536], P(None, ('blk', 'head'))
- next_avg_w_shared_out: float32 [1024, 1536], P(None, ('blk', 'head'))
Inputs may be any that keep to these rules, and one draw needn't show every extreme that they name: `doc_starts`: never falling; each value is the position of its document's first token, at or before the token's own position; documents are at most 3072 long and one is exactly 3072 long; a multiple of 3072 starts a document unless it lies strictly inside a document of 3072 tokens. `routes`: each row names 6 different experts. `expert_slots`: within the 128 tokens of one device, the pairs that name one expert hold distinct cells 0 to 15; a pair holds -1 only when all 16 cells of its expert are taken by other pairs of that device; some expert's cells are all taken on every device.
All inputs are finite; a program needn't handle non-finite values.
Results may differ from a plain program's by a relative error of at most 0.025.
Values may be sent and summed in bfloat16 or wider, within the bound.
No kernel may reach another device: no remote copies, remote signals or barrier semaphores. Data moves between devices by JAX's collectives and lax.ppermute only.
A program may use at most 384 MiB of HBM per device.

v0:
```python
import jax
import jax.numpy as jnp
from jax import lax
from jax.sharding import PartitionSpec as P

QUERY_HEADS = 12
KEY_VALUE_HEADS = 4
HEAD_SIZE = 128
EXPERTS = 64
FE = 512
FS = 1024
CAP = 16


NORM_EPSILON = 1e-05
MASKED_SCORE = -1e30
LEARN_RATE = 0.001
MOMENTUM = 0.5
DECAY = 0.5


def shifted(value, axis, steps):
    count = lax.axis_size(axis)
    initial, last = (max(0, -steps), min(count, count - steps))
    return lax.ppermute(value, axis, [(source, source + steps) for source in range(initial, last)])


def from_behind(shard, axis, by):
    devices = lax.axis_size(axis)
    return lax.ppermute(shard, axis, [(i, (i + by) % devices) for i in range(devices)])


def silu_slope(values):
    sigmoid = jax.nn.sigmoid(values)
    return sigmoid * (1.0 + values * (1.0 - sigmoid))


def norm_forward(values, gain_row):
    inverse = lax.rsqrt(jnp.mean(values * values, axis=-1, keepdims=True) + NORM_EPSILON)
    return (values * inverse * gain_row, inverse)


def norm_backward(values, inverse, gain_row, upstream):
    scaled = gain_row * upstream
    gain_grad = jnp.sum(upstream * values * inverse, axis=0)
    input_grad = inverse * scaled - values * inverse**3 * jnp.mean(
        scaled * values, axis=-1, keepdims=True
    )
    return (input_grad, gain_grad)


def contract_rows(left_side, right_side):
    return lax.dot_general(
        left_side, right_side, (((0,), (0,)), ((), ())), preferred_element_type=jnp.float32
    )


def contract_cols(left_side, right_side):
    return lax.dot_general(
        left_side, right_side, (((1,), (1,)), ((), ())), preferred_element_type=jnp.float32
    )


def gather_dense(norm_gains, qkv_projection_weight, w_out, w_router, w_shared_in, w_shared_out):
    return (
        lax.all_gather(norm_gains.astype(jnp.bfloat16), ("blk", "head"), axis=1, tiled=True),
        lax.all_gather(
            qkv_projection_weight.astype(jnp.bfloat16), ("blk", "head"), axis=0, tiled=True
        ),
        lax.all_gather(w_out.astype(jnp.bfloat16), ("blk", "head"), axis=1, tiled=True),
        lax.all_gather(w_router.astype(jnp.bfloat16), ("blk", "head"), axis=0, tiled=True),
        lax.all_gather(w_shared_in.astype(jnp.bfloat16), ("blk", "head"), axis=0, tiled=True),
        lax.all_gather(w_shared_out.astype(jnp.bfloat16), ("blk", "head"), axis=1, tiled=True),
    )


def gather_experts(w_moe_in, w_moe_out):
    return (
        lax.all_gather(w_moe_in.astype(jnp.bfloat16), "head", axis=1, tiled=True),
        lax.all_gather(w_moe_out.astype(jnp.bfloat16), "head", axis=2, tiled=True),
    )


def send_to_experts(buffer):
    return lax.all_to_all(buffer, "blk", split_axis=0, concat_axis=0, tiled=True)


def send_from_experts(buffer):
    return lax.all_to_all(buffer, "blk", split_axis=0, concat_axis=0, tiled=True)


def pass_keys(key_pair):
    return shifted(key_pair, "blk", 1)


def pass_key_grads(key_grads):
    return from_behind(key_grads.astype(jnp.bfloat16), "blk", 1).astype(key_grads.dtype)


def block_scores(queries, key_rows, doc_starts, key_index):
    group_rows = queries.shape[0]
    own_index = lax.axis_index("blk")
    query_pos = own_index * group_rows + jnp.arange(group_rows, dtype=jnp.int32)
    key_pos = key_index * group_rows + jnp.arange(group_rows, dtype=jnp.int32)
    visible = (key_pos[None, :] <= query_pos[:, None]) & (key_pos[None, :] >= doc_starts[:, None])
    scores = jnp.einsum(
        "qrd,kd->qrk", queries, key_rows, preferred_element_type=jnp.float32
    ) * HEAD_SIZE ** (-0.5)
    return (scores, visible[:, None, :])


def block_live(doc_starts, key_index, group_rows):
    own_index = lax.axis_index("blk")
    return (
        (key_index >= 0)
        & (key_index <= own_index)
        & ((key_index + 1) * group_rows - 1 >= doc_starts[0])
    )


def attend_forward(queries, key_pair, doc_starts):
    group_rows, heads_per_group, head_dim = queries.shape
    cycle_size = lax.axis_size("blk")
    own_index = lax.axis_index("blk")

    def absorb(softmax_state, pair_now, key_index):

        def active(current):
            running, row_total, weighted = current
            scores, visible = block_scores(queries, pair_now[0], doc_starts, key_index)
            scores = jnp.where(visible, scores, MASKED_SCORE)
            new_max = jnp.maximum(running, jnp.max(scores, axis=-1))
            weights = jnp.where(visible, jnp.exp(scores - new_max[:, :, None]), 0.0)
            factor = jnp.exp(running - new_max)
            row_total = row_total * factor + jnp.sum(weights, axis=-1)
            weighted = weighted * factor[:, :, None] + jnp.einsum(
                "qrk,kd->qrd",
                weights.astype(jnp.bfloat16),
                pair_now[1],
                preferred_element_type=jnp.float32,
            )
            return (new_max, row_total, weighted)

        return lax.cond(
            block_live(doc_starts, key_index, group_rows),
            active,
            lambda unchanged: unchanged,
            softmax_state,
        )

    softmax_state = (
        jnp.full((group_rows, heads_per_group), MASKED_SCORE, jnp.float32),
        jnp.zeros((group_rows, heads_per_group), jnp.float32),
        jnp.zeros((group_rows, heads_per_group, head_dim), jnp.float32),
    )
    softmax_state = absorb(softmax_state, key_pair, own_index)

    def cycle_turn(turn_index, cycle_carry):
        state_now, pair_now = cycle_carry
        pair_now = pass_keys(pair_now)
        key_index = own_index - turn_index
        return (absorb(state_now, pair_now, key_index), pair_now)

    softmax_state, final_pair = lax.fori_loop(1, cycle_size, cycle_turn, (softmax_state, key_pair))
    running, row_total, weighted = softmax_state
    return (weighted / row_total[:, :, None], running + jnp.log(row_total), key_pair)


def attend_backward(queries, key_pair, grad_heads, attn_rows, log_total, doc_starts):
    group_rows, heads_per_group, head_dim = queries.shape
    cycle_size = lax.axis_size("blk")
    own_index = lax.axis_index("blk")
    score_scale = HEAD_SIZE ** (-0.5)
    row_delta = jnp.sum(grad_heads.astype(jnp.float32) * attn_rows, axis=-1)

    def absorb(grad_pair, pair_now, key_index):

        def active(current):
            grad_queries, grad_keys = current
            scores, visible = block_scores(queries, pair_now[0], doc_starts, key_index)
            weights = jnp.where(visible, jnp.exp(scores - log_total[:, :, None]), 0.0)
            grad_weights = jnp.einsum(
                "qrd,kd->qrk", grad_heads, pair_now[1], preferred_element_type=jnp.float32
            )
            grad_scores = (weights * (grad_weights - row_delta[:, :, None])).astype(jnp.bfloat16)
            grad_queries = grad_queries + score_scale * jnp.einsum(
                "qrk,kd->qrd", grad_scores, pair_now[0], preferred_element_type=jnp.float32
            )
            key_part = score_scale * jnp.einsum(
                "qrk,qrd->kd", grad_scores, queries, preferred_element_type=jnp.float32
            )
            value_part = jnp.einsum(
                "qrk,qrd->kd",
                weights.astype(jnp.bfloat16),
                grad_heads,
                preferred_element_type=jnp.float32,
            )
            return (grad_queries, grad_keys + jnp.stack([key_part, value_part]))

        return lax.cond(
            block_live(doc_starts, key_index, group_rows),
            active,
            lambda unchanged: unchanged,
            grad_pair,
        )

    query_zero = jnp.zeros((group_rows, heads_per_group, head_dim), jnp.float32)
    block_zero = jnp.zeros((2, group_rows, head_dim), jnp.float32)
    grad_pair = absorb((query_zero, block_zero), key_pair, own_index)

    def cycle_turn(turn_index, cycle_carry):
        grad_queries, grad_keys, pair_now = cycle_carry
        pair_now = pass_keys(pair_now)
        grad_keys = pass_key_grads(grad_keys)
        key_index = own_index - turn_index
        grad_queries, grad_keys = absorb((grad_queries, grad_keys), pair_now, key_index)
        return (grad_queries, grad_keys, pair_now)

    grad_queries, grad_keys, final_pair = lax.fori_loop(
        1, cycle_size, cycle_turn, (grad_pair[0], grad_pair[1], key_pair)
    )
    return (grad_queries, pass_key_grads(grad_keys))


def apply_update(weight, gradient, moment, average):
    moment_new = MOMENTUM * moment + gradient
    change = -LEARN_RATE * (gradient + MOMENTUM * moment_new)
    weight_new = weight + change
    average_new = DECAY * average + (1.0 - DECAY) * weight_new
    return (gradient, weight_new, moment_new, average_new, change)


def local(
    tokens,
    cotangent,
    doc_starts,
    routes,
    expert_slots,
    norm_gains,
    qkv_projection_weight,
    w_out,
    w_router,
    w_moe_in,
    w_moe_out,
    w_shared_in,
    w_shared_out,
    mom_norm_gains,
    momentum_qkv_weight,
    mom_w_out,
    mom_w_router,
    mom_w_moe_in,
    mom_w_moe_out,
    mom_w_shared_in,
    mom_w_shared_out,
    avg_norm_gains,
    averaged_qkv_weight,
    avg_w_out,
    avg_w_router,
    avg_w_moe_in,
    avg_w_moe_out,
    avg_w_shared_in,
    avg_w_shared_out,
):
    stream_token_rows, model_width = tokens.shape
    heads_per_group = QUERY_HEADS // KEY_VALUE_HEADS
    cycle_size = lax.axis_size("blk")
    local_experts = w_moe_in.shape[0]
    cell_count = EXPERTS * CAP
    gain_full, qkv_full, out_full, router_full, shared_in_full, shared_out_full = gather_dense(
        norm_gains, qkv_projection_weight, w_out, w_router, w_shared_in, w_shared_out
    )
    gain_rows = gain_full.astype(jnp.float32)
    normed_one, inverse_one = norm_forward(tokens, gain_rows[0])
    input_one = normed_one.astype(jnp.bfloat16)
    projected_rows = jnp.dot(input_one, qkv_full, preferred_element_type=jnp.float32).astype(
        jnp.bfloat16
    )
    regrouped = lax.all_to_all(
        projected_rows.reshape(
            stream_token_rows, KEY_VALUE_HEADS, (heads_per_group + 2) * HEAD_SIZE
        ),
        "head",
        split_axis=1,
        concat_axis=0,
        tiled=True,
    )
    group_rows = regrouped.shape[0]
    queries = regrouped[:, 0, : heads_per_group * HEAD_SIZE].reshape(
        group_rows, heads_per_group, HEAD_SIZE
    )
    key_pair = (
        regrouped[:, 0, heads_per_group * HEAD_SIZE :]
        .reshape(group_rows, 2, HEAD_SIZE)
        .transpose(1, 0, 2)
    )
    attn_rows, log_total, whole_pairs = attend_forward(queries, key_pair, doc_starts)
    attn_back = lax.all_to_all(
        attn_rows.astype(jnp.bfloat16).reshape(group_rows, 1, heads_per_group * HEAD_SIZE),
        "head",
        split_axis=0,
        concat_axis=1,
        tiled=True,
    )
    attn_tokens = attn_back.reshape(stream_token_rows, QUERY_HEADS * HEAD_SIZE)
    mixed_rows = tokens + jnp.dot(attn_tokens, out_full, preferred_element_type=jnp.float32)
    normed_two, inverse_two = norm_forward(mixed_rows, gain_rows[1])
    input_two = normed_two.astype(jnp.bfloat16)
    router_logits = jnp.dot(input_two, router_full, preferred_element_type=jnp.float32)
    gate_probs = jax.nn.softmax(jnp.take_along_axis(router_logits, routes, axis=1), axis=-1)
    cell_codes = jnp.where(expert_slots >= 0, routes * CAP + expert_slots, -1)
    cell_match = cell_codes[:, :, None] == jnp.arange(cell_count, dtype=jnp.int32)[None, None, :]
    dispatch_table = jnp.any(cell_match, axis=1).astype(jnp.bfloat16)
    combine_weights = jnp.sum(jnp.where(cell_match, gate_probs[:, :, None], 0.0), axis=1).astype(
        jnp.bfloat16
    )
    outgoing = contract_rows(dispatch_table, input_two).astype(jnp.bfloat16)
    received = send_to_experts(outgoing.reshape(cycle_size, local_experts, CAP, model_width))
    moe_in_full, moe_out_full = gather_experts(w_moe_in, w_moe_out)
    gate_up = jnp.einsum(
        "bjcd,jdf->bjcf", received, moe_in_full, preferred_element_type=jnp.float32
    )
    expert_gate = gate_up[..., :FE]
    expert_up = gate_up[..., FE:]
    expert_hidden = (jax.nn.silu(expert_gate) * expert_up).astype(jnp.bfloat16)
    expert_rows = jnp.einsum(
        "bjcf,jfd->bjcd", expert_hidden, moe_out_full, preferred_element_type=jnp.float32
    ).astype(jnp.bfloat16)
    returned = send_from_experts(expert_rows).reshape(cell_count, model_width)
    expert_out = jnp.dot(combine_weights, returned, preferred_element_type=jnp.float32)
    shared_gate_up = jnp.dot(input_two, shared_in_full, preferred_element_type=jnp.float32)
    shared_gate = shared_gate_up[:, :FS]
    shared_up = shared_gate_up[:, FS:]
    shared_hidden = (jax.nn.silu(shared_gate) * shared_up).astype(jnp.bfloat16)
    shared_rows = jnp.dot(shared_hidden, shared_out_full, preferred_element_type=jnp.float32)
    output = mixed_rows + shared_rows + expert_out
    back_dense = gather_dense(
        norm_gains, qkv_projection_weight, w_out, w_router, w_shared_in, w_shared_out
    )
    back_experts = gather_experts(w_moe_in, w_moe_out)
    qkv_back = back_dense[1]
    out_back = back_dense[2]
    router_back = back_dense[3]
    shared_in_back = back_dense[4]
    shared_out_back = back_dense[5]
    grad_out_low = cotangent.astype(jnp.bfloat16)
    grad_w_shared_out = contract_rows(shared_hidden, grad_out_low)
    grad_shared_hidden = contract_cols(grad_out_low, shared_out_back)
    grad_shared_gate_up = jnp.concatenate(
        [
            grad_shared_hidden * shared_up * silu_slope(shared_gate),
            grad_shared_hidden * jax.nn.silu(shared_gate),
        ],
        axis=-1,
    ).astype(jnp.bfloat16)
    grad_w_shared_in = contract_rows(input_two, grad_shared_gate_up)
    grad_combine = contract_cols(grad_out_low, returned)
    grad_gates = jnp.sum(jnp.where(cell_match, grad_combine[:, None, :], 0.0), axis=-1)
    grad_chosen = gate_probs * (
        grad_gates - jnp.sum(gate_probs * grad_gates, axis=-1, keepdims=True)
    )
    route_match = routes[:, :, None] == jnp.arange(EXPERTS, dtype=jnp.int32)[None, None, :]
    grad_logits = jnp.sum(jnp.where(route_match, grad_chosen[:, :, None], 0.0), axis=1).astype(
        jnp.bfloat16
    )
    grad_w_router = contract_rows(input_two, grad_logits)
    grad_expert_rows = contract_rows(combine_weights, grad_out_low).astype(jnp.bfloat16)
    grad_received = send_to_experts(
        grad_expert_rows.reshape(cycle_size, local_experts, CAP, model_width)
    )
    grad_w_moe_out = jnp.einsum(
        "bjcf,bjcd->jfd", expert_hidden, grad_received, preferred_element_type=jnp.float32
    )
    grad_hidden = jnp.einsum(
        "bjcd,jfd->bjcf", grad_received, back_experts[1], preferred_element_type=jnp.float32
    )
    grad_gate_up = jnp.concatenate(
        [grad_hidden * expert_up * silu_slope(expert_gate), grad_hidden * jax.nn.silu(expert_gate)],
        axis=-1,
    ).astype(jnp.bfloat16)
    grad_w_moe_in = jnp.einsum(
        "bjcd,bjcf->jdf", received, grad_gate_up, preferred_element_type=jnp.float32
    )
    grad_outgoing = jnp.einsum(
        "bjcf,jdf->bjcd", grad_gate_up, back_experts[0], preferred_element_type=jnp.float32
    ).astype(jnp.bfloat16)
    grad_returned = send_from_experts(grad_outgoing).reshape(cell_count, model_width)
    grad_input_two = (
        contract_cols(grad_shared_gate_up, shared_in_back)
        + contract_cols(grad_logits, router_back)
        + jnp.dot(dispatch_table, grad_returned, preferred_element_type=jnp.float32)
    )
    grad_mixed_norm, grad_gain_two = norm_backward(
        mixed_rows, inverse_two, gain_rows[1], grad_input_two
    )
    grad_mixed = cotangent + grad_mixed_norm
    grad_mixed_low = grad_mixed.astype(jnp.bfloat16)
    grad_w_out = contract_rows(attn_tokens, grad_mixed_low)
    attention_gradient = contract_cols(grad_mixed_low, out_back).astype(jnp.bfloat16)
    grad_heads = lax.all_to_all(
        attention_gradient.reshape(stream_token_rows, KEY_VALUE_HEADS, heads_per_group * HEAD_SIZE),
        "head",
        split_axis=1,
        concat_axis=0,
        tiled=True,
    ).reshape(group_rows, heads_per_group, HEAD_SIZE)
    grad_queries, grad_keys = attend_backward(
        queries, key_pair, grad_heads, attn_rows, log_total, doc_starts
    )
    grad_pack = jnp.concatenate(
        [
            grad_queries.reshape(group_rows, heads_per_group * HEAD_SIZE),
            grad_keys.transpose(1, 0, 2).reshape(group_rows, 2 * HEAD_SIZE),
        ],
        axis=-1,
    ).astype(jnp.bfloat16)
    grad_projected = lax.all_to_all(
        grad_pack.reshape(group_rows, 1, (heads_per_group + 2) * HEAD_SIZE),
        "head",
        split_axis=0,
        concat_axis=1,
        tiled=True,
    ).reshape(stream_token_rows, KEY_VALUE_HEADS * (heads_per_group + 2) * HEAD_SIZE)
    grad_w_qkv = contract_rows(input_one, grad_projected)
    grad_input_one = contract_cols(grad_projected, qkv_back)
    grad_token_norm, grad_gain_one = norm_backward(
        tokens, inverse_one, gain_rows[0], grad_input_one
    )
    grad_tokens = grad_mixed + grad_token_norm
    grad_gains_full = jnp.stack([grad_gain_one, grad_gain_two])
    gain_part, qkv_part, out_part, router_part, shared_in_part, shared_out_part = (
        lax.psum_scatter(grad_gains_full, ("blk", "head"), scatter_dimension=1, tiled=True),
        lax.psum_scatter(grad_w_qkv, ("blk", "head"), scatter_dimension=0, tiled=True),
        lax.psum_scatter(grad_w_out, ("blk", "head"), scatter_dimension=1, tiled=True),
        lax.psum_scatter(grad_w_router, ("blk", "head"), scatter_dimension=0, tiled=True),
        lax.psum_scatter(grad_w_shared_in, ("blk", "head"), scatter_dimension=0, tiled=True),
        lax.psum_scatter(grad_w_shared_out, ("blk", "head"), scatter_dimension=1, tiled=True),
    )
    moe_in_part, moe_out_part = (
        lax.psum_scatter(
            grad_w_moe_in.astype(jnp.bfloat16), "head", scatter_dimension=1, tiled=True
        ).astype(jnp.float32),
        lax.psum_scatter(
            grad_w_moe_out.astype(jnp.bfloat16), "head", scatter_dimension=2, tiled=True
        ).astype(jnp.float32),
    )
    gains_new = apply_update(norm_gains, gain_part, mom_norm_gains, avg_norm_gains)
    qkv_new = apply_update(
        qkv_projection_weight, qkv_part, momentum_qkv_weight, averaged_qkv_weight
    )
    out_new = apply_update(w_out, out_part, mom_w_out, avg_w_out)
    router_new = apply_update(w_router, router_part, mom_w_router, avg_w_router)
    moe_in_new = apply_update(w_moe_in, moe_in_part, mom_w_moe_in, avg_w_moe_in)
    moe_out_new = apply_update(w_moe_out, moe_out_part, mom_w_moe_out, avg_w_moe_out)
    shared_in_new = apply_update(w_shared_in, shared_in_part, mom_w_shared_in, avg_w_shared_in)
    shared_out_new = apply_update(w_shared_out, shared_out_part, mom_w_shared_out, avg_w_shared_out)
    return (
        output,
        grad_tokens,
        gains_new[0],
        gains_new[1],
        gains_new[2],
        gains_new[3],
        qkv_new[0],
        qkv_new[1],
        qkv_new[2],
        qkv_new[3],
        out_new[0],
        out_new[1],
        out_new[2],
        out_new[3],
        router_new[0],
        router_new[1],
        router_new[2],
        router_new[3],
        moe_in_new[0],
        moe_in_new[1],
        moe_in_new[2],
        moe_in_new[3],
        moe_out_new[0],
        moe_out_new[4],
        moe_out_new[2],
        moe_out_new[3],
        shared_in_new[0],
        shared_in_new[1],
        shared_in_new[2],
        shared_in_new[3],
        shared_out_new[0],
        shared_out_new[1],
        shared_out_new[2],
        shared_out_new[3],
    )


def solution(mesh):
    in_specs = (
        P(("blk", "head"), None),
        P(("blk", "head"), None),
        P("blk"),
        P(("blk", "head"), None),
        P(("blk", "head"), None),
        P(None, ("blk", "head")),
        P(("blk", "head"), None),
        P(None, ("blk", "head")),
        P(("blk", "head"), None),
        P("blk", "head", None),
        P("blk", None, "head"),
        P(("blk", "head"), None),
        P(None, ("blk", "head")),
        P(None, ("blk", "head")),
        P(("blk", "head"), None),
        P(None, ("blk", "head")),
        P(("blk", "head"), None),
        P("blk", "head", None),
        P("blk", None, "head"),
        P(("blk", "head"), None),
        P(None, ("blk", "head")),
        P(None, ("blk", "head")),
        P(("blk", "head"), None),
        P(None, ("blk", "head")),
        P(("blk", "head"), None),
        P("blk", "head", None),
        P("blk", None, "head"),
        P(("blk", "head"), None),
        P(None, ("blk", "head")),
    )
    out_specs = (
        P(("blk", "head"), None),
        P(("blk", "head"), None),
        P(None, ("blk", "head")),
        P(None, ("blk", "head")),
        P(None, ("blk", "head")),
        P(None, ("blk", "head")),
        P(("blk", "head"), None),
        P(("blk", "head"), None),
        P(("blk", "head"), None),
        P(("blk", "head"), None),
        P(None, ("blk", "head")),
        P(None, ("blk", "head")),
        P(None, ("blk", "head")),
        P(None, ("blk", "head")),
        P(("blk", "head"), None),
        P(("blk", "head"), None),
        P(("blk", "head"), None),
        P(("blk", "head"), None),
        P("blk", "head", None),
        P("blk", "head", None),
        P("blk", "head", None),
        P("blk", "head", None),
        P("blk", None, "head"),
        P("blk", None, "head"),
        P("blk", None, "head"),
        P("blk", None, "head"),
        P(("blk", "head"), None),
        P(("blk", "head"), None),
        P(("blk", "head"), None),
        P(("blk", "head"), None),
        P(None, ("blk", "head")),
        P(None, ("blk", "head")),
        P(None, ("blk", "head")),
        P(None, ("blk", "head")),
    )
    return jax.shard_map(local, mesh=mesh, in_specs=in_specs, out_specs=out_specs, check_vma=False)
```

profile of v0, /device:TPU:0, one launch (start us, length us, event | category | flops | bytes accessed | tf_op | source)
XLA Modules:
  0.0 1956.1 jit_solution(11108662747167398060)
XLA Ops:
  28.2 43.7 %all-gather = bf16[32,48,2]{1,2,0:T(2,128)(2,1)S(1)} all-gather(bf16[1,48,2]{1,2,0:T(2,128)(2,1)S(1)} %convert_bitcast_fusion), channel_id=1, replica_groups=mesh['blk'=8,'head'=4] {'blk','head'}, dimensions={0}, use_global_device_ids=true | all-gather | bytes 6336 | tf_op jit(solution)/shard_map/all_gather | solution.py:66
  72.7 16.4 all-gather.8.cloned.1.call-done
  116.7 108.3 %while.40 = (s32[]{:T(128)}, f32[512,3]{0,1:T(4,128)}, f32[512,3]{0,1:T(4,128)S(1)}, f32[512,3,128]{2,0,1:T(8,128)S(1)}, bf16[2,512,128]{2,1,0:T(8,128)(2,1)}, /...) while((s32[]{:T(128)}, f32[512,3]{0,1:T(4,128)}, ...), condition=%wide.region_10.11_spmd, body=%wide.region_5.10_spmd.sunk | while | flops 414060544 | bytes 14399963 | solution.py:164
  251.3 26.2 %all-to-all-start.2 = ((bf16[8,8,16,1536]{3,2,1,0:T(8,128)(2,1)}), bf16[8,8,16,1536]{3,2,1,0:T(8,128)(2,1)}, u32[]{:S(2)}, u32[]{:S(2)}) async-start(bf16[8,8,16,1536]{3,2,1,0:T(8,128)(2,1)} %bitcast.227), calls=%async_computation.2 | async-start | bytes 6291456 | tf_op jit(solution)/shard_map/all_to_all | solution.py:85
  283.6 62.1 %all-gather.14.cloned.1.call-done = bf16[1024,1536]{0,1:T(8,128)(2,1)} async-done(((bf16[1024,48]{0,1:T(8,128)(2,1)}), bf16[1024,1536]{0,1:T(8,128)(2,1)}) %all-gather.14.cloned.1.call-update) | async-done | bytes 3145744 | tf_op jit(solution)/shard_map/all_gather | solution.py:73
  357.1 143.0 %all-gather.16.cloned.1.call-done = bf16[8,1536,1024]{2,1,0:T(8,128)(2,1)} async-done(((bf16[8,384,1024]{2,1,0:T(8,128)(2,1)}), bf16[8,1536,1024]{2,1,0:T(8,128)(2,1)}) %all-gather.16.cloned.1.call-update) | async-done | bytes 25165840 | tf_op jit(solution)/shard_map/all_gather | solution.py:79
  515.4 68.6 %all-gather.18.cloned.1.call-done = bf16[8,512,1536]{2,1,0:T(8,128)(2,1)} async-done(((bf16[8,512,384]{2,1,0:T(8,128)(2,1)}), bf16[8,512,1536]{2,1,0:T(8,128)(2,1)}) %all-gather.18.cloned.1.call-update) | async-done | bytes 12582928 | tf_op jit(solution)/shard_map/all_gather | solution.py:80
  598.5 97.1 %all_gather.36 = bf16[1536,64]{1,0:T(8,128)(2,1)S(1)} all-gather(bf16[48,64]{1,0:T(8,128)(2,1)S(1)} %convert_element_type.189), channel_id=1, replica_groups=mesh['blk'=8,'head'=4] {'blk','head'}, dimensions={0}, use_global_device_ids=true | all-gather | bytes 202752 | tf_op jit(solution)/shard_map/all_gather | solution.py:71
  712.3 20.9 %all-to-all-start.4 = ((bf16[8,8,16,1536]{3,2,1,0:T(8,128)(2,1)}), bf16[8,8,16,1536]{3,2,1,0:T(8,128)(2,1)}, u32[]{:S(2)}, u32[]{:S(2)}) async-start(bf16[8,8,16,1536]{3,2,1,0:T(8,128)(2,1)} %bitcast.229), calls=%async_computation.4 | async-start | bytes 6291456 | tf_op jit(solution)/shard_map/all_to_all | solution.py:85
  740.8 78.7 %all-to-all-done.4 = bf16[8,8,16,1536]{3,2,1,0:T(8,128)(2,1)} async-done(((bf16[8,8,16,1536]{3,2,1,0:T(8,128)(2,1)}), bf16[8,8,16,1536]{3,2,1,0:T(8,128)(2,1)}, u32[]{:S(2)}, u32[]{:S(2)}) %all-to-all-start.4) | async-done | bytes 3145760 | tf_op jit(solution)/shard_map/all_to_all | solution.py:85
  819.5 12.4 fusion.92
  831.9 15.1 fusion.79
  862.6 88.3 %all-to-all-done.5 = bf16[8,8,16,1536]{3,2,1,0:T(8,128)(2,1)} async-done(((bf16[8,8,16,1536]{3,2,1,0:T(8,128)(2,1)}), bf16[8,8,16,1536]{3,2,1,0:T(8,128)(2,1)}, u32[]{:S(2)}, u32[]{:S(2)}) %all-to-all-start.5) | async-done | bytes 3145760 | tf_op jit(solution)/shard_map/all_to_all | solution.py:89
  976.7 113.9 %while.41 = (s32[]{:T(128)}, f32[512,3,128]{2,0,1:T(8,128)S(1)}, f32[2,512,128]{2,1,0:T(8,128)S(1)}, bf16[2,512,128]{2,1,0:T(8,128)(2,1)}, s32[]{:T(128)}, /*ind...) while((s32[]{:T(128)}, f32[512,3,128]{2,0,1:T(8,128)S(1)}, ...), condition=%wide.region_26.27_spmd, body=%wide.region_23.26_spmd.sunk | while | flops 1016267776 | bytes 26403404 | solution.py:219
  1143.9 17.3 copy.258
  1161.2 12.9 copy.263
  1183.2 13.6 bitcast_convert_fusion
  1213.6 97.0 %reduce-scatter.25.cloned.1.call-done = f32[48,2]{1,0:T(8,128)} async-done(((f32[1536,2]{1,0:T(8,128)}), f32[48,2]{1,0:T(8,128)}) %reduce-scatter.25.cloned.1.call-update) | async-done | bytes 400
  1312.0 141.0 %reduce-scatter.15.cloned.1.call-done = f32[1536,48]{0,1:T(8,128)} async-done(((f32[1536,1536]{0,1:T(8,128)}), f32[1536,48]{0,1:T(8,128)}) %reduce-scatter.15.cloned.1.call-update) | async-done | bytes 294928 | tf_op jit(solution)/shard_map/reduce_scatter | solution.py:433
  1454.9 99.6 %reduce-scatter.27.cloned.1.call-done = bf16[384,4096]{1,0:T(8,128)(2,1)} async-done(((bf16[1536,4096]{1,0:T(8,128)(2,1)}), bf16[384,4096]{1,0:T(8,128)(2,1)}) %reduce-scatter.27.cloned.1.call-update) | async-done | bytes 3145744
  1563.3 15.8 add_multiply_fusion.1
  1579.2 152.8 %reduce-scatter.13.cloned.1.call-done = f32[48,2560]{1,0:T(8,128)} async-done(((f32[1536,2560]{1,0:T(8,128)}), f32[48,2560]{1,0:T(8,128)}) %reduce-scatter.13.cloned.1.call-update) | async-done | bytes 491536 | tf_op jit(solution)/shard_map/reduce_scatter | solution.py:432
  1734.6 180.7 %reduce-scatter.19.cloned.1.call-done = bf16[8,384,1024]{2,1,0:T(8,128)(2,1)} async-done(((bf16[8,1536,1024]{2,1,0:T(8,128)(2,1)}), bf16[8,384,1024]{2,1,0:T(8,128)(2,1)}) %reduce-scatter.19.cloned.1.call-update) | async-done | bytes 6291472 | tf_op jit(solution)/shard_map/reduce_scatter | solution.py:439
  1915.3 33.7 %add_multiply_fusion = (f32[8,384,1024]{2,1,0:T(8,128)}, f32[8,384,1024]{2,1,0:T(8,128)}, f32[8,384,1024]{2,1,0:T(8,128)}, f32[8,384,1024]{2,1,0:T(8,128)}) fusion(f32[8,384,1024]{2,1,0:T(8,128)} %param.66, f32[8,384,1024]{2,1,0:T(8,128)} %param.50, f32[8,384,1024]{2,1,0:T(8,128)} %param.58, bf16[8,384,1024]{2,1,0:T(8,128)(2,1)} %reduce-scatter.19.cloned.1.call-done), kind=kLoop, calls=%fused_computation.95 | loop fusion | flops 28311552 | bytes 94371840 | tf_op jit(solution)/shard_map/add | solution.py:229
  (375 shorter events, 504.3 us)
Async XLA Ops:
  7.2 81.9 %all-gather.8.cloned.1.call-start = ((), (), s32[]{:S(2)}) async-start(), calls=%async_computation.16 | async-start | bytes 8110080 | tf_op jit(solution)/shard_map/all_gather | solution.py:67
  9.0 235.1 %all-gather.10.cloned.1.call-start = ((), (), s32[]{:S(2)}) async-start(), calls=%async_computation.17 | async-start | bytes 4866048 | tf_op jit(solution)/shard_map/all_gather | solution.py:70
  10.7 268.1 %all-gather.12.cloned.1.call-start = ((), (), s32[]{:S(2)}) async-start(), calls=%async_computation.18 | async-start | bytes 6488064 | tf_op jit(solution)/shard_map/all_gather | solution.py:72
  12.5 333.1 %all-gather.14.cloned.1.call-start = ((), (), s32[]{:S(2)}) async-start(), calls=%async_computation.19 | async-start | bytes 3244032 | tf_op jit(solution)/shard_map/all_gather | solution.py:73
  14.2 485.9 %all-gather.16.cloned.1.call-start = ((), (), s32[]{:S(2)}) async-start(), calls=%async_computation.20 | async-start | bytes 31457280 | tf_op jit(solution)/shard_map/all_gather | solution.py:79
  22.5 561.5 %all-gather.18.cloned.1.call-start = ((), (), s32[]{:S(2)}) async-start(), calls=%async_computation.21 | async-start | bytes 15728640 | tf_op jit(solution)/shard_map/all_gather | solution.py:80
  127.9 23.3 %collective-permute-start = (bf16[2,512,128]{2,1,0:T(8,128)(2,1)}, bf16[2,512,128]{2,1,0:T(8,128)(2,1)S(1)}, u32[]{:S(2)}, u32[]{:S(2)}) collective-permute-start(bf16[2,512,128]{2,1,0:T(8,128)(2,1)} %get-tuple-element.982), channel_id=1, source_target_pairs={{0,4},{4,8},{8,12},{12,16},{16,20},{20,24},{24,28},{1,5},{5,9},{9,... | collective-permute-start | bytes 786440 | tf_op jit(solution)/shard_map/while/body/eval_jaxpr/ppermute | solution.py:25
  185.4 15.9 collective-permute-start
  202.0 22.2 %collective-permute-start = (bf16[2,512,128]{2,1,0:T(8,128)(2,1)}, bf16[2,512,128]{2,1,0:T(8,128)(2,1)S(1)}, u32[]{:S(2)}, u32[]{:S(2)}) collective-permute-start(bf16[2,512,128]{2,1,0:T(8,128)(2,1)} %get-tuple-element.982), channel_id=1, source_target_pairs={{0,4},{4,8},{8,12},{12,16},{16,20},{20,24},{24,28},{1,5},{5,9},{9,... | collective-permute-start | bytes 786440 | tf_op jit(solution)/shard_map/while/body/eval_jaxpr/ppermute | solution.py:25
  251.3 105.8 %all-to-all-start.2 = ((bf16[8,8,16,1536]{3,2,1,0:T(8,128)(2,1)}), bf16[8,8,16,1536]{3,2,1,0:T(8,128)(2,1)}, u32[]{:S(2)}, u32[]{:S(2)}) async-start(bf16[8,8,16,1536]{3,2,1,0:T(8,128)(2,1)} %bitcast.227), calls=%async_computation.2 | async-start | bytes 6291456 | tf_op jit(solution)/shard_map/all_to_all | solution.py:85
  277.6 924.4 %reduce-scatter.23.cloned.1.call-start = ((), (), s32[]{:S(2)}) async-start(), calls=%async_computation.27 | async-start | bytes 6488064 | tf_op jit(solution)/shard_map/reduce_scatter | solution.py:436
  592.6 109.4 %all-to-all-start.3 = ((bf16[8,8,16,1536]{3,2,1,0:T(8,128)(2,1)}), bf16[8,8,16,1536]{3,2,1,0:T(8,128)(2,1)}, u32[]{:S(2)}, u32[]{:S(2)}) async-start(bf16[8,8,16,1536]{3,2,1,0:T(8,128)(2,1)} %copy.225), calls=%async_computation.3 | async-start | bytes 6291456 | tf_op jit(solution)/shard_map/all_to_all | solution.py:89
  712.3 107.2 %all-to-all-start.4 = ((bf16[8,8,16,1536]{3,2,1,0:T(8,128)(2,1)}), bf16[8,8,16,1536]{3,2,1,0:T(8,128)(2,1)}, u32[]{:S(2)}, u32[]{:S(2)}) async-start(bf16[8,8,16,1536]{3,2,1,0:T(8,128)(2,1)} %bitcast.229), calls=%async_computation.4 | async-start | bytes 6291456 | tf_op jit(solution)/shard_map/all_to_all | solution.py:85
  733.2 470.9 %reduce-scatter.21.cloned.1.call-start = ((), (), s32[]{:S(2)}) async-start(), calls=%async_computation.26 | async-start | bytes 12976128 | tf_op jit(solution)/shard_map/reduce_scatter | solution.py:435
  850.8 100.0 %all-to-all-start.5 = ((bf16[8,8,16,1536]{3,2,1,0:T(8,128)(2,1)}), bf16[8,8,16,1536]{3,2,1,0:T(8,128)(2,1)}, u32[]{:S(2)}, u32[]{:S(2)}) async-start(bf16[8,8,16,1536]{3,2,1,0:T(8,128)(2,1)} %copy.228), calls=%async_computation.5 | async-start | bytes 6291456 | tf_op jit(solution)/shard_map/all_to_all | solution.py:89
  1022.7 15.9 collective-permute-start.1
  1040.5 16.6 collective-permute-start.2
  1058.0 15.9 collective-permute-start.2
  1106.6 103.3 %reduce-scatter.17.cloned.1.call-start = ((), (), s32[]{:S(2)}) async-start(), calls=%async_computation.24 | async-start | bytes 811008 | tf_op jit(solution)/shard_map/reduce_scatter | solution.py:434
  1107.8 202.8 %reduce-scatter.25.cloned.1.call-start = ((), (), s32[]{:S(2)}) async-start(), calls=%async_computation.28 | async-start | bytes 811008
  1127.9 325.1 %reduce-scatter.15.cloned.1.call-start = ((), (), s32[]{:S(2)}) async-start(), calls=%async_computation.23 | async-start | bytes 9732096 | tf_op jit(solution)/shard_map/reduce_scatter | solution.py:433
  1133.1 421.4 %reduce-scatter.27.cloned.1.call-start = ((), (), s32[]{:S(2)}) async-start(), calls=%async_computation.29 | async-start | bytes 15728640
  1174.1 557.8 %reduce-scatter.13.cloned.1.call-start = ((), (), s32[]{:S(2)}) async-start(), calls=%async_computation.22 | async-start | bytes 16220160 | tf_op jit(solution)/shard_map/reduce_scatter | solution.py:432
  1182.0 733.4 %reduce-scatter.19.cloned.1.call-start = ((), (), s32[]{:S(2)}) async-start(), calls=%async_computation.25 | async-start | bytes 31457280 | tf_op jit(solution)/shard_map/reduce_scatter | solution.py:439
  (71 other events, 2642.2 us)
Sparse Core Ops, SparseCore 0:
  11.5 77.6 all-gather.7
  92.6 70.8 all-gather.9
  167.0 75.4 all-gather.11
  245.8 99.7 all-gather.13
  347.7 152.3 all-gather.15
  502.1 81.8 all-gather.17
  590.2 129.4 reduce-scatter.22
  741.1 199.6 reduce-scatter.20
  1113.0 96.5 reduce-scatter.16
  1215.2 95.3 reduce-scatter.24
  1317.6 135.2 reduce-scatter.14
  1456.0 98.5 reduce-scatter.26
  1561.1 170.7 reduce-scatter.12
  1734.4 180.9 reduce-scatter.18
where the time goes:
time: 1970 us; the launch traced here: 1960 us
  waiting for transfers between devices  1270 us (64%)
  starting transfers between devices  160 us (8%)
  matrix products  156 us (8%)
  blocking collectives  141 us (7%)
  other arithmetic  104 us (5%)
  local copies, waits for them, and re-layouts  97.3 us (5%)
    unnamed x16, waiting for transfers between devices  197 us
    reduce_scatter x1, waiting for transfers between devices, local(): lax.psum_scatter(grad_w_moe_in.astype(jnp.bfloat16), 'head', scatter_dime...  181 us
    reduce_scatter x1, waiting for transfers between devices, local(): lax.psum_scatter(grad_w_qkv, ('blk', 'head'), scatter_dimension=0, tiled=...  153 us
    all_gather x1, waiting for transfers between devices, gather_experts(): lax.all_gather(w_moe_in.astype(jnp.bfloat16), 'head', axis=1, tiled=True)  143 us
    reduce_scatter x1, waiting for transfers between devices, local(): lax.psum_scatter(grad_w_out, ('blk', 'head'), scatter_dimension=1, tiled=...  141 us
    all_gather x1, blocking collectives, gather_dense(): lax.all_gather(w_router.astype(jnp.bfloat16), ('blk', 'head'), axis=0, ti...  97.1 us
    all_to_all x2, waiting for transfers between devices, send_from_experts(): lax.all_to_all(buffer, 'blk', split_axis=0, concat_axis=0, tiled=True)  88.3 us
    all_to_all x2, waiting for transfers between devices, send_to_experts(): lax.all_to_all(buffer, 'blk', split_axis=0, concat_axis=0, tiled=True)  80.9 us
  transfers between devices with their start and end apart: 44, of which 33 were waited for; matrix products, arithmetic and copies ran while one was open for 16% of the time, Pallas kernels for 0%

commit v1 on v0

v1 whole, which is shorter than its diff:
```python
import jax
import jax.numpy as jnp
from jax import lax
from jax.sharding import PartitionSpec as P

QUERY_HEADS = 12
KEY_VALUE_HEADS = 4
HEAD_SIZE = 128
EXPERTS = 64
FE = 512
FS = 1024
CAP = 16


NORM_EPSILON = 1e-05
MASKED_SCORE = -1e30
LEARN_RATE = 0.001
MOMENTUM = 0.5
DECAY = 0.5


def silu_slope(values):
    sigmoid = jax.nn.sigmoid(values)
    return sigmoid * (1.0 + values * (1.0 - sigmoid))


def norm_forward(values, gain_row):
    inverse = lax.rsqrt(jnp.mean(values * values, axis=-1, keepdims=True) + NORM_EPSILON)
    return (values * inverse * gain_row, inverse)


def norm_backward(values, inverse, gain_row, upstream):
    scaled = gain_row * upstream
    gain_grad = jnp.sum(upstream * values * inverse, axis=0)
    input_grad = inverse * scaled - values * inverse**3 * jnp.mean(
        scaled * values, axis=-1, keepdims=True
    )
    return (input_grad, gain_grad)


def contract_rows(left_side, right_side):
    return lax.dot_general(
        left_side, right_side, (((0,), (0,)), ((), ())), preferred_element_type=jnp.float32
    )


def contract_cols(left_side, right_side):
    return lax.dot_general(
        left_side, right_side, (((1,), (1,)), ((), ())), preferred_element_type=jnp.float32
    )


def low(values):
    return values.astype(jnp.bfloat16)


def gather_rows(shard, axis):
    return lax.all_gather(shard, axis, axis=0, tiled=True)


def scatter_rows(partial, axis):
    return lax.psum_scatter(partial, axis, scatter_dimension=0, tiled=True)


def exchange(pieces, axis):
    return lax.all_to_all(pieces, axis, split_axis=0, concat_axis=0, tiled=True)


def visible_keys(doc_starts, key_index):
    group_rows = doc_starts.shape[0]
    own_index = lax.axis_index("blk")
    query_pos = own_index * group_rows + jnp.arange(group_rows, dtype=jnp.int32)
    key_pos = key_index * group_rows + jnp.arange(group_rows, dtype=jnp.int32)
    return (key_pos[None, :] <= query_pos[:, None]) & (key_pos[None, :] >= doc_starts[:, None])


def block_scores(queries, keys, visible):
    scores = jnp.einsum("rqd,kd->rqk", queries, keys, preferred_element_type=jnp.float32)
    return jnp.where(visible[None], scores * HEAD_SIZE ** (-0.5), MASKED_SCORE)


def key_block(pairs, key_index, group_rows):
    block = lax.dynamic_slice_in_dim(pairs, key_index * group_rows, group_rows, 0)
    return (block[:, :HEAD_SIZE], block[:, HEAD_SIZE:])


def attend_forward(queries, pairs, doc_starts):
    heads_per_group, group_rows, head_dim = queries.shape
    own_index = lax.axis_index("blk")

    def absorb(key_index, state):
        running, row_total, weighted = state
        keys, values = key_block(pairs, key_index, group_rows)
        scores = block_scores(queries, keys, visible_keys(doc_starts, key_index))
        new_max = jnp.maximum(running, jnp.max(scores, axis=-1, keepdims=True))
        weights = jnp.where(scores > 0.5 * MASKED_SCORE, jnp.exp(scores - new_max), 0.0)
        factor = jnp.exp(running - new_max)
        row_total = row_total * factor + jnp.sum(weights, axis=-1, keepdims=True)
        weighted = weighted * factor + jnp.einsum(
            "rqk,kd->rqd", low(weights), values, preferred_element_type=jnp.float32
        )
        return (new_max, row_total, weighted)

    state = (
        jnp.full((heads_per_group, group_rows, 1), MASKED_SCORE, jnp.float32),
        jnp.zeros((heads_per_group, group_rows, 1), jnp.float32),
        jnp.zeros((heads_per_group, group_rows, head_dim), jnp.float32),
    )
    first = doc_starts[0] // group_rows
    running, row_total, weighted = lax.fori_loop(first, own_index + 1, absorb, state)
    return (weighted / row_total, running + jnp.log(row_total))


def attend_backward(queries, pairs, grad_heads, attn_rows, log_total, doc_starts):
    heads_per_group, group_rows, head_dim = queries.shape
    own_index = lax.axis_index("blk")
    score_scale = HEAD_SIZE ** (-0.5)
    row_delta = jnp.sum(grad_heads.astype(jnp.float32) * attn_rows, axis=-1, keepdims=True)

    def absorb(key_index, grads):
        grad_queries, grad_pairs = grads
        keys, values = key_block(pairs, key_index, group_rows)
        scores = block_scores(queries, keys, visible_keys(doc_starts, key_index))
        weights = jnp.exp(scores - log_total)
        grad_weights = jnp.einsum(
            "rqd,kd->rqk", grad_heads, values, preferred_element_type=jnp.float32
        )
        grad_scores = low(weights * (grad_weights - row_delta))
        grad_queries = grad_queries + score_scale * jnp.einsum(
            "rqk,kd->rqd", grad_scores, keys, preferred_element_type=jnp.float32
        )
        key_part = score_scale * jnp.einsum(
            "rqk,rqd->kd", grad_scores, queries, preferred_element_type=jnp.float32
        )
        value_part = jnp.einsum(
            "rqk,rqd->kd", low(weights), grad_heads, preferred_element_type=jnp.float32
        )
        part = low(jnp.concatenate([key_part, value_part], axis=-1))
        grad_pairs = lax.dynamic_update_slice_in_dim(grad_pairs, part, key_index * group_rows, 0)
        return (grad_queries, grad_pairs)

    grads = (jnp.zeros(queries.shape, jnp.float32), jnp.zeros(pairs.shape, jnp.bfloat16))
    first = doc_starts[0] // group_rows
    return lax.fori_loop(first, own_index + 1, absorb, grads)


def apply_update(weight, gradient, moment, average):
    moment_new = MOMENTUM * moment + gradient
    change = -LEARN_RATE * (gradient + MOMENTUM * moment_new)
    weight_new = weight + change
    average_new = DECAY * average + (1.0 - DECAY) * weight_new
    return (gradient, weight_new, moment_new, average_new, change)


def local(
    tokens,
    cotangent,
    doc_starts,
    routes,
    expert_slots,
    norm_gains,
    qkv_projection_weight,
    w_out,
    w_router,
    w_moe_in,
    w_moe_out,
    w_shared_in,
    w_shared_out,
    mom_norm_gains,
    momentum_qkv_weight,
    mom_w_out,
    mom_w_router,
    mom_w_moe_in,
    mom_w_moe_out,
    mom_w_shared_in,
    mom_w_shared_out,
    avg_norm_gains,
    averaged_qkv_weight,
    avg_w_out,
    avg_w_router,
    avg_w_moe_in,
    avg_w_moe_out,
    avg_w_shared_in,
    avg_w_shared_out,
):
    rows, model_width = tokens.shape
    heads = lax.axis_size("head")
    blocks = lax.axis_size("blk")
    per_group = QUERY_HEADS // KEY_VALUE_HEADS
    query_width = per_group * HEAD_SIZE
    pair_width = 2 * HEAD_SIZE
    shared_width = FS // heads
    slice_width = model_width // heads
    local_experts = w_moe_in.shape[0]
    weight_rows = w_router.shape[0]
    group_rows = rows * heads
    cell_count = EXPERTS * CAP
    own_head = lax.axis_index("head")

    def split_heads(weight):
        return low(weight).reshape(weight_rows, heads, -1)

    def every_head(weight):
        return jnp.broadcast_to(low(weight)[:, None, :], (weight_rows, heads, weight.shape[1]))

    def spread(pieces):
        packed = jnp.concatenate(pieces, axis=-1).transpose(1, 0, 2)
        return gather_rows(exchange(packed, "head").reshape(heads * weight_rows, -1), "blk")

    def collect(partial):
        mine = scatter_rows(low(partial), "blk").reshape(heads, weight_rows, -1)
        return exchange(mine, "head").transpose(1, 0, 2).astype(jnp.float32)

    first_pack = spread([split_heads(qkv_projection_weight), every_head(norm_gains.T)])
    inverse_one = lax.rsqrt(jnp.mean(tokens * tokens, axis=-1, keepdims=True) + NORM_EPSILON)
    unit_one = gather_rows(low(tokens * inverse_one), "head")
    qkv_width = query_width + pair_width
    qkv_cols = first_pack[:, :qkv_width]
    gain_rows = first_pack[:, qkv_width:].astype(jnp.float32).T
    input_one = low(unit_one.astype(jnp.float32) * gain_rows[0])
    projected = low(jnp.dot(input_one, qkv_cols, preferred_element_type=jnp.float32))
    queries = projected[:, :query_width].reshape(group_rows, per_group, HEAD_SIZE)
    queries = queries.transpose(1, 0, 2)
    pairs = gather_rows(projected[:, query_width:], "blk")
    second_pack = spread(
        [
            split_heads(w_out.T),
            split_heads(w_shared_in[:, :FS]),
            split_heads(w_shared_in[:, FS:]),
            split_heads(w_shared_out.T),
            every_head(w_router),
        ]
    )
    out_cols = second_pack[:, :query_width]
    shared_in_cols = second_pack[:, query_width : query_width + 2 * shared_width]
    shared_out_cols = second_pack[:, query_width + 2 * shared_width :][:, :shared_width]
    router_full = second_pack[:, query_width + 3 * shared_width :]
    grad_low = low(cotangent)
    grad_low_all = gather_rows(grad_low, "head")
    moe_in_low = low(w_moe_in)
    moe_out_low = low(w_moe_out)

    attn_rows, log_total = attend_forward(queries, pairs, doc_starts)
    attn_flat = low(attn_rows).transpose(1, 0, 2).reshape(group_rows, query_width)
    mixed_rows = tokens + scatter_rows(low(contract_cols(attn_flat, out_cols)), "head").astype(
        jnp.float32
    )
    normed_two, inverse_two = norm_forward(mixed_rows, gain_rows[1])
    input_two = low(normed_two)
    input_two_all = gather_rows(input_two, "head")

    router_logits = jnp.dot(input_two, router_full, preferred_element_type=jnp.float32)
    route_match = routes[:, :, None] == jnp.arange(EXPERTS, dtype=jnp.int32)[None, None, :]
    gate_probs = jax.nn.softmax(
        jnp.sum(jnp.where(route_match, router_logits[:, None, :], 0.0), axis=-1), axis=-1
    )
    cell_codes = jnp.where(expert_slots >= 0, routes * CAP + expert_slots, -1)
    cell_match = cell_codes[:, :, None] == jnp.arange(cell_count, dtype=jnp.int32)[None, None, :]
    dispatch_table = low(jnp.any(cell_match, axis=1))
    combine_weights = low(jnp.sum(jnp.where(cell_match, gate_probs[:, :, None], 0.0), axis=1))

    def to_owners(table, values):
        cells = low(contract_rows(table, values))
        return cells.reshape(blocks, local_experts * CAP, heads, slice_width).transpose(0, 2, 1, 3)

    outgoing = jnp.concatenate(
        [to_owners(dispatch_table, input_two), to_owners(combine_weights, grad_low)], axis=-1
    ).reshape(blocks * heads, local_experts, CAP, 2 * slice_width)
    received = exchange(outgoing, ("blk", "head"))
    cells_in = received[..., :slice_width]
    grads_in = received[..., slice_width:]
    gate_up_part = jnp.einsum(
        "secf,efn->escn", cells_in, moe_in_low, preferred_element_type=jnp.float32
    )
    grad_hidden_part = jnp.einsum(
        "secf,ekf->esck", grads_in, moe_out_low, preferred_element_type=jnp.float32
    )
    expert_part = low(jnp.concatenate([gate_up_part, grad_hidden_part], axis=-1))
    expert_sum = scatter_rows(expert_part.reshape(-1, 3 * FE), "head").astype(jnp.float32)
    expert_gate = expert_sum[:, :FE]
    expert_up = expert_sum[:, FE : 2 * FE]
    grad_hidden = expert_sum[:, 2 * FE :]
    expert_acts = low(
        jnp.concatenate(
            [
                jax.nn.silu(expert_gate) * expert_up,
                grad_hidden * expert_up * silu_slope(expert_gate),
                grad_hidden * jax.nn.silu(expert_gate),
            ],
            axis=-1,
        )
    )
    acts_all = gather_rows(expert_acts, "head").reshape(
        local_experts, blocks * heads, CAP, 3 * FE
    )
    hidden_all = acts_all[..., :FE]
    grad_gate_up = acts_all[..., FE:]
    rows_part = jnp.einsum(
        "esck,ekf->secf", hidden_all, moe_out_low, preferred_element_type=jnp.float32
    )
    grad_cells_part = jnp.einsum(
        "escn,efn->secf", grad_gate_up, moe_in_low, preferred_element_type=jnp.float32
    )
    back = exchange(
        jnp.concatenate([low(rows_part), low(grad_cells_part)], axis=-1), ("blk", "head")
    )
    back = back.reshape(blocks, heads, local_experts * CAP, 2, slice_width)
    back = back.transpose(3, 0, 2, 1, 4).reshape(2, cell_count, model_width)
    returned = back[0]
    grad_returned = back[1]
    moe_in_grad = jnp.einsum(
        "secf,escn->efn", cells_in, grad_gate_up, preferred_element_type=jnp.float32
    )
    moe_out_grad = jnp.einsum(
        "esck,secf->ekf", hidden_all, grads_in, preferred_element_type=jnp.float32
    )

    shared_gate_up = jnp.dot(input_two_all, shared_in_cols, preferred_element_type=jnp.float32)
    shared_gate = shared_gate_up[:, :shared_width]
    shared_up = shared_gate_up[:, shared_width:]
    shared_hidden = low(jax.nn.silu(shared_gate) * shared_up)
    grad_shared_hidden = jnp.dot(grad_low_all, shared_out_cols, preferred_element_type=jnp.float32)
    grad_shared_gate_up = low(
        jnp.concatenate(
            [
                grad_shared_hidden * shared_up * silu_slope(shared_gate),
                grad_shared_hidden * jax.nn.silu(shared_gate),
            ],
            axis=-1,
        )
    )
    shared_part = jnp.concatenate(
        [
            low(contract_cols(shared_hidden, shared_out_cols)),
            low(contract_cols(grad_shared_gate_up, shared_in_cols)),
        ],
        axis=-1,
    )
    shared_sum = scatter_rows(shared_part, "head").astype(jnp.float32)

    expert_out = jnp.dot(combine_weights, returned, preferred_element_type=jnp.float32)
    output = mixed_rows + shared_sum[:, :model_width] + expert_out
    grad_combine = contract_cols(grad_low, returned)
    grad_gates = jnp.sum(jnp.where(cell_match, grad_combine[:, None, :], 0.0), axis=-1)
    grad_chosen = gate_probs * (
        grad_gates - jnp.sum(gate_probs * grad_gates, axis=-1, keepdims=True)
    )
    grad_logits = low(jnp.sum(jnp.where(route_match, grad_chosen[:, :, None], 0.0), axis=1))
    grad_input_two = (
        shared_sum[:, model_width:]
        + contract_cols(grad_logits, router_full)
        + jnp.dot(dispatch_table, grad_returned, preferred_element_type=jnp.float32)
    )
    grad_mixed_norm, grad_gain_two = norm_backward(
        mixed_rows, inverse_two, gain_rows[1], grad_input_two
    )
    grad_mixed = cotangent + grad_mixed_norm
    mixed_pack = gather_rows(jnp.concatenate([low(grad_mixed), grad_logits], axis=-1), "head")
    grad_mixed_all = mixed_pack[:, :model_width]
    grad_logits_own = lax.dynamic_slice_in_dim(
        mixed_pack[:, model_width:], own_head * (EXPERTS // heads), EXPERTS // heads, 1
    )
    second_grads = collect(
        jnp.concatenate(
            [
                contract_rows(grad_mixed_all, attn_flat),
                contract_rows(input_two_all, grad_shared_gate_up),
                contract_rows(grad_low_all, shared_hidden),
                contract_rows(input_two_all, grad_logits_own),
            ],
            axis=-1,
        )
    )

    def own_columns(grads, start, width):
        return grads[:, :, start : start + width].reshape(weight_rows, heads * width)

    out_part = own_columns(second_grads, 0, query_width).T
    shared_in_part = jnp.concatenate(
        [
            own_columns(second_grads, query_width, shared_width),
            own_columns(second_grads, query_width + shared_width, shared_width),
        ],
        axis=-1,
    )
    shared_out_part = own_columns(second_grads, query_width + 2 * shared_width, shared_width).T
    router_part = own_columns(second_grads, query_width + 3 * shared_width, EXPERTS // heads)

    grad_heads = low(jnp.dot(grad_mixed_all, out_cols, preferred_element_type=jnp.float32))
    grad_heads = grad_heads.reshape(group_rows, per_group, HEAD_SIZE).transpose(1, 0, 2)
    grad_queries, grad_pairs = attend_backward(
        queries, pairs, grad_heads, attn_rows, log_total, doc_starts
    )
    pair_parts = exchange(grad_pairs.reshape(blocks, group_rows, pair_width), "blk")
    grad_projected = jnp.concatenate(
        [
            low(grad_queries).transpose(1, 0, 2).reshape(group_rows, query_width),
            low(jnp.sum(pair_parts.astype(jnp.float32), axis=0)),
        ],
        axis=-1,
    )
    input_grad_part = contract_cols(grad_projected, qkv_cols)
    gain_one_part = jnp.sum(input_grad_part * unit_one.astype(jnp.float32), axis=0)
    gain_parts = jnp.stack([gain_one_part, grad_gain_two], axis=-1)
    first_grads = collect(
        jnp.concatenate([contract_rows(input_one, grad_projected), gain_parts], axis=-1)
    )
    qkv_part = own_columns(first_grads, 0, qkv_width)
    gain_part = jnp.sum(first_grads[:, :, qkv_width:], axis=1).T
    grad_input_one = scatter_rows(low(input_grad_part), "head").astype(jnp.float32)
    grad_token_norm, unused_gain = norm_backward(tokens, inverse_one, gain_rows[0], grad_input_one)
    grad_tokens = grad_mixed + grad_token_norm

    gains_new = apply_update(norm_gains, gain_part, mom_norm_gains, avg_norm_gains)
    qkv_new = apply_update(
        qkv_projection_weight, qkv_part, momentum_qkv_weight, averaged_qkv_weight
    )
    out_new = apply_update(w_out, out_part, mom_w_out, avg_w_out)
    router_new = apply_update(w_router, router_part, mom_w_router, avg_w_router)
    moe_in_new = apply_update(w_moe_in, moe_in_grad, mom_w_moe_in, avg_w_moe_in)
    moe_out_new = apply_update(w_moe_out, moe_out_grad, mom_w_moe_out, avg_w_moe_out)
    shared_in_new = apply_update(w_shared_in, shared_in_part, mom_w_shared_in, avg_w_shared_in)
    shared_out_new = apply_update(w_shared_out, shared_out_part, mom_w_shared_out, avg_w_shared_out)
    return (
        output,
        grad_tokens,
        gains_new[0],
        gains_new[1],
        gains_new[2],
        gains_new[3],
        qkv_new[0],
        qkv_new[1],
        qkv_new[2],
        qkv_new[3],
        out_new[0],
        out_new[1],
        out_new[2],
        out_new[3],
        router_new[0],
        router_new[1],
        router_new[2],
        router_new[3],
        moe_in_new[0],
        moe_in_new[1],
        moe_in_new[2],
        moe_in_new[3],
        moe_out_new[0],
        moe_out_new[4],
        moe_out_new[2],
        moe_out_new[3],
        shared_in_new[0],
        shared_in_new[1],
        shared_in_new[2],
        shared_in_new[3],
        shared_out_new[0],
        shared_out_new[1],
        shared_out_new[2],
        shared_out_new[3],
    )


def solution(mesh):
    in_specs = (
        P(("blk", "head"), None),
        P(("blk", "head"), None),
        P("blk"),
        P(("blk", "head"), None),
        P(("blk", "head"), None),
        P(None, ("blk", "head")),
        P(("blk", "head"), None),
        P(None, ("blk", "head")),
        P(("blk", "head"), None),
        P("blk", "head", None),
        P("blk", None, "head"),
        P(("blk", "head"), None),
        P(None, ("blk", "head")),
        P(None, ("blk", "head")),
        P(("blk", "head"), None),
        P(None, ("blk", "head")),
        P(("blk", "head"), None),
        P("blk", "head", None),
        P("blk", None, "head"),
        P(("blk", "head"), None),
        P(None, ("blk", "head")),
        P(None, ("blk", "head")),
        P(("blk", "head"), None),
        P(None, ("blk", "head")),
        P(("blk", "head"), None),
        P("blk", "head", None),
        P("blk", None, "head"),
        P(("blk", "head"), None),
        P(None, ("blk", "head")),
    )
    out_specs = (
        P(("blk", "head"), None),
        P(("blk", "head"), None),
        P(None, ("blk", "head")),
        P(None, ("blk", "head")),
        P(None, ("blk", "head")),
        P(None, ("blk", "head")),
        P(("blk", "head"), None),
        P(("blk", "head"), None),
        P(("blk", "head"), None),
        P(("blk", "head"), None),
        P(None, ("blk", "head")),
        P(None, ("blk", "head")),
        P(None, ("blk", "head")),
        P(None, ("blk", "head")),
        P(("blk", "head"), None),
        P(("blk", "head"), None),
        P(("blk", "head"), None),
        P(("blk", "head"), None),
        P("blk", "head", None),
        P("blk", "head", None),
        P("blk", "head", None),
        P("blk", "head", None),
        P("blk", None, "head"),
        P("blk", None, "head"),
        P("blk", None, "head"),
        P("blk", None, "head"),
        P(("blk", "head"), None),
        P(("blk", "head"), None),
        P(("blk", "head"), None),
        P(("blk", "head"), None),
        P(None, ("blk", "head")),
        P(None, ("blk", "head")),
        P(None, ("blk", "head")),
        P(None, ("blk", "head")),
    )
    return jax.shard_map(local, mesh=mesh, in_specs=in_specs, out_specs=out_specs, check_vma=False)
```

time: 1970 us -> 1240 us (0.63)
  waiting for transfers between devices: 1270 us -> 672 us
  starting transfers between devices: 160 us -> 88.3 us
  other arithmetic: 104 us -> 53.9 us
    reduce_scatter x6, waiting for transfers between devices: 474 us -> 266 us  [scatter_rows(): return lax.psum_scatter(partial, axis, scatter_dimension=0, tiled=True)]
    unnamed x16 -> x14, waiting for transfers between devices: 197 us -> 1.4 us
    all_to_all x0 -> x2, blocking collectives: none -> 153 us  [exchange(): return lax.all_to_all(pieces, axis, split_axis=0, concat_axis=0, tiled=True)]
    all_gather x2 -> x0, blocking collectives: 141 us -> none  [the longest x1 97.1 us: gather_dense(): lax.all_gather(w_router.astype(jnp.bfloat16), ('blk', 'head'), axis=0, ti...]
    ppermute x22 -> x0, waiting for transfers between devices: 111 us -> none  [the longest x8 62.3 us: from_behind(): lax.ppermute(shard, axis, [(i, (i + by) % devices) for i in range(devices)])]
    all_to_all x8 -> x5, waiting for transfers between devices: 200 us -> 91.4 us  [exchange(): return lax.all_to_all(pieces, axis, split_axis=0, concat_axis=0, tiled=True)]
    ppermute x22 -> x0, starting transfers between devices: 86.6 us -> none  [the longest x14 73.6 us: shifted(): lax.ppermute(value, axis, [(source, source + steps) for source in range(i...]
    add x8 -> x6, other arithmetic: 60.6 us -> 7.09 us  [apply_update(): average_new = DECAY * average + (1.0 - DECAY) * weight_new]
  transfers between devices with their start and end apart: 44 -> 19, of which waited for: 33 -> 17; matrix products, arithmetic and copies ran while one was open for 16% -> 11% of each run, Pallas kernels for 0% -> 0%
where the time goes in v1:
time: 1240 us; the launch traced here: 1230 us
  waiting for transfers between devices  672 us (54%)
  blocking collectives  153 us (12%)
  matrix products  142 us (11%)
  local copies, waits for them, and re-layouts  99.1 us (8%)
  starting transfers between devices  88.3 us (7%)
  other arithmetic  53.9 us (4%)
  between operations  18.4 us (1%)
    all_gather x8, waiting for transfers between devices, gather_rows(): return lax.all_gather(shard, axis, axis=0, tiled=True)  313 us
    reduce_scatter x6, waiting for transfers between devices, scatter_rows(): return lax.psum_scatter(partial, axis, scatter_dimension=0, tiled=True)  266 us
    all_to_all x2, blocking collectives, exchange(): return lax.all_to_all(pieces, axis, split_axis=0, concat_axis=0, tiled=True)  153 us
    all_to_all x5, waiting for transfers between devices, exchange(): return lax.all_to_all(pieces, axis, split_axis=0, concat_axis=0, tiled=True)  91.4 us
    all_to_all x5, starting transfers between devices, exchange(): return lax.all_to_all(pieces, axis, split_axis=0, concat_axis=0, tiled=True)  86.6 us
    dot_general x1, matrix products, local(): jnp.einsum('secf,escn->efn', cells_in, grad_gate_up, preferred_element_ty...  33.5 us
    slice x2, local copies, waits for them, and re-layouts, local(): grad_returned = back[1]  25.4 us
  transfers between devices with their start and end apart: 19, of which 17 were waited for; matrix products, arithmetic and copies ran while one was open for 11% of the time, Pallas kernels for 0%

profile of v1, /device:TPU:0, one launch (start us, length us, event | category | flops | bytes accessed | tf_op | source)
XLA Modules:
  0.0 1227.7 jit_solution(5420099805909550715)
XLA Ops:
  9.5 10.5 all_to_all.35
  22.2 50.5 %all-gather.11.cloned.1.call-done = bf16[1536,642]{1,0:T(8,128)(2,1)} async-done(((bf16[192,642]{1,0:T(8,128)(2,1)}), bf16[1536,642]{1,0:T(8,128)(2,1)}) %all-gather.11.cloned.1.call-update) | async-done | bytes 1972240 | tf_op jit(solution)/shard_map/all_gather | solution.py:58
  74.8 18.2 %all-gather.9.cloned.1.call-done = bf16[512,1536]{1,0:T(8,128)(2,1)} async-done(((bf16[128,1536]{1,0:T(8,128)(2,1)}), bf16[512,1536]{1,0:T(8,128)(2,1)}) %all-gather.9.cloned.1.call-update) | async-done | bytes 1572880 | tf_op jit(solution)/shard_map/all_gather | solution.py:58
  112.7 33.9 %all-gather.13.cloned.1.call-done = bf16[4096,256]{1,0:T(8,128)(2,1)} async-done(((bf16[512,256]{1,0:T(8,128)(2,1)}), bf16[4096,256]{1,0:T(8,128)(2,1)}) %all-gather.13.cloned.1.call-update) | async-done | bytes 2097168 | tf_op jit(solution)/shard_map/all_gather | solution.py:58
  156.4 60.9 %all-gather.15.cloned.1.call-done = bf16[1536,1216]{1,0:T(8,128)(2,1)} async-done(((bf16[192,1216]{1,0:T(8,128)(2,1)}), bf16[1536,1216]{1,0:T(8,128)(2,1)}) %all-gather.15.cloned.1.call-update) | async-done | bytes 3735568 | tf_op jit(solution)/shard_map/all_gather | solution.py:58
  223.2 24.3 %reduce-scatter.11.cloned.1.call-done = bf16[128,1536]{1,0:T(8,128)(2,1)} async-done(((bf16[512,1536]{1,0:T(8,128)(2,1)}), bf16[128,1536]{1,0:T(8,128)(2,1)}) %reduce-scatter.11.cloned.1.call-update) | async-done | bytes 393232 | tf_op jit(solution)/shard_map/reduce_scatter | solution.py:62
  266.7 143.0 %all_to_all.36 = bf16[32,8,16,768]{3,2,1,0:T(8,128)(2,1)S(1)} all-to-all(bf16[32,8,16,768]{3,2,1,0:T(8,128)(2,1)S(1)} %bitcast.281), channel_id=1, replica_groups=mesh['blk'=8,'head'=4] {'blk','head'}, dimensions={0} | all-to-all | bytes 12582912 | tf_op jit(solution)/shard_map/all_to_all | solution.py:66
  415.7 11.3 convolution_convert_fusion
  437.6 98.8 %reduce-scatter.15.cloned.1.call-done = bf16[1024,1536]{1,0:T(8,128)(2,1)} async-done(((bf16[4096,1536]{1,0:T(8,128)(2,1)}), bf16[1024,1536]{1,0:T(8,128)(2,1)}) %reduce-scatter.15.cloned.1.call-update) | async-done | bytes 3145744 | tf_op jit(solution)/shard_map/reduce_scatter | solution.py:62
  543.2 81.5 %all-gather.21.cloned.1.call-done = bf16[4096,1536]{1,0:T(8,128)(2,1)} async-done(((bf16[1024,1536]{1,0:T(8,128)(2,1)}), bf16[4096,1536]{1,0:T(8,128)(2,1)}) %all-gather.21.cloned.1.call-update) | async-done | bytes 12582928 | tf_op jit(solution)/shard_map/all_gather | solution.py:58
  624.7 11.5 convert_bitcast_fusion
  655.3 47.2 %all-gather.19.cloned.1.call-done = bf16[512,1536]{1,0:T(8,128)(2,1)} async-done(((bf16[128,1536]{1,0:T(8,128)(2,1)}), bf16[512,1536]{1,0:T(8,128)(2,1)}) %all-gather.19.cloned.1.call-update) | async-done | bytes 1572880 | tf_op jit(solution)/shard_map/all_gather | solution.py:58
  709.3 51.5 %reduce-scatter.13.cloned.1.call-done = bf16[128,3072]{1,0:T(8,128)(2,1)} async-done(((bf16[512,3072]{1,0:T(8,128)(2,1)}), bf16[128,3072]{1,0:T(8,128)(2,1)}) %reduce-scatter.13.cloned.1.call-update) | async-done | bytes 786448 | tf_op jit(solution)/shard_map/reduce_scatter | solution.py:62
  763.3 28.3 %all-to-all-done.3 = bf16[32,8,16,768]{3,2,1,0:T(8,128)(2,1)} async-done(((bf16[32,8,16,768]{3,2,1,0:T(8,128)(2,1)}), bf16[32,8,16,768]{3,2,1,0:T(8,128)(2,1)}, u32[]{:S(2)}, u32[]{:S(2)}) %all-to-all-start.3) | async-done | bytes 6291488 | tf_op jit(solution)/shard_map/all_to_all | solution.py:66
  791.5 12.8 %reshape.414 = bf16[8,4,128,2,384]{4,3,2,1,0:T(2,128)(2,1)} reshape(bf16[32,8,16,768]{3,2,1,0:T(8,128)(2,1)} %all-to-all-done.3) | data formatting | bytes 12582912 | tf_op jit(solution)/shard_map/reshape | solution.py:307
  804.3 15.4 %fusion.142 = (bf16[1,8,128,4,384]{4,0,2,3,1:T(2,128)(2,1)}, bf16[1,8,128,4,384]{4,0,2,3,1:T(2,128)(2,1)}) fusion(bf16[2,8,128,4,384]{4,0,2,3,1:T(2,128)(2,1)} %bitcast.278), kind=kLoop, calls=%fused_computation.237 | loop fusion | bytes 12582912 | tf_op jit(solution)/shard_map/slice | solution.py:310
  853.7 21.0 %all-gather.23.cloned.1.call-done = bf16[512,1600]{1,0:T(8,128)(2,1)} async-done(((bf16[128,1600]{1,0:T(8,128)(2,1)}), bf16[512,1600]{1,0:T(8,128)(2,1)}) %all-gather.23.cloned.1.call-update) | async-done | bytes 1638416 | tf_op jit(solution)/shard_map/all_gather | solution.py:58
  880.5 11.1 while.27
  895.5 71.5 %all-to-all-start.4 = ((bf16[8,512,256]{1,2,0:T(8,128)(2,1)}), bf16[8,512,256]{1,2,0:T(8,128)(2,1)S(1)}, u32[]{:S(2)}, u32[]{:S(2)}) async-start(bf16[8,512,256]{1,2,0:T(8,128)(2,1)} %copy.326), calls=%async_computation.7 | async-start | bytes 4194304 | tf_op jit(solution)/shard_map/all_to_all | solution.py:66
  968.2 47.4 %all-to-all-done.4 = bf16[8,512,256]{1,2,0:T(8,128)(2,1)S(1)} async-done(((bf16[8,512,256]{1,2,0:T(8,128)(2,1)}), bf16[8,512,256]{1,2,0:T(8,128)(2,1)S(1)}, u32[]{:S(2)}, u32[]{:S(2)}) %all-to-all-start.4) | async-done | bytes 2097184 | tf_op jit(solution)/shard_map/all_to_all | solution.py:66
  1037.1 33.5 %add_multiply_fusion = (f32[8,384,1024]{2,1,0:T(8,128)}, f32[8,384,1024]{2,1,0:T(8,128)}, f32[8,384,1024]{2,1,0:T(8,128)}, f32[8,384,1024]{2,1,0:T(8,128)}) fusion(f32[8,384,1024]{2,1,0:T(8,128)} %param.58, f32[8,384,1024]{2,1,0:T(8,128)} %param.42, f32[8,384,1024]{2,1,0:T(8,128)} %param.50, bf16[8,32,16,1536]{3,2,1,0:T(8,128)(2,1)} %bitcast.296, ...), kind=kOutput, calls=%fused_computation.51 | convolution fusion | flops 3246391296 | bytes 99614720 | tf_op jit(solution)/shard_map/secf,escn->efn/dot_general | solution.py:311
  1076.1 17.1 %add_multiply_fusion.1 = (f32[8,512,384]{2,1,0:T(8,128)}, f32[8,512,384]{2,1,0:T(8,128)}, f32[8,512,384]{2,1,0:T(8,128)}, f32[8,512,384]{2,1,0:T(8,128)}) fusion(f32[8,512,384]{2,1,0:T(8,128)} %param.59, f32[8,512,384]{2,1,0:T(8,128)} %param.43, f32[8,512,384]{2,1,0:T(8,128)} %param.51, bf16[32,8,16,384]{3,2,1,0:T(8,128)(2,1)} %copy-done.14, ...), kind=kOutput, calls=%fused_computation.63 | convolution fusion | flops 1623195648 | bytes 51380224 | tf_op jit(solution)/shard_map/esck,secf->ekf/dot_general | solution.py:314
  1098.5 37.8 %reduce-scatter.21.cloned.1.call-done = bf16[192,1168]{1,0:T(8,128)(2,1)} async-done(((bf16[1536,1168]{1,0:T(8,128)(2,1)}), bf16[192,1168]{1,0:T(8,128)(2,1)}) %reduce-scatter.21.cloned.1.call-update) | async-done | bytes 448528 | tf_op jit(solution)/shard_map/reduce_scatter | solution.py:62
  1154.9 53.9 %reduce-scatter.19.cloned.1.call-done = bf16[192,642]{1,0:T(8,128)(2,1)} async-done(((bf16[1536,642]{1,0:T(8,128)(2,1)}), bf16[192,642]{1,0:T(8,128)(2,1)}) %reduce-scatter.19.cloned.1.call-update) | async-done | bytes 246544 | tf_op jit(solution)/shard_map/reduce_scatter | solution.py:62
  (380 shorter events, 233.8 us)
Async XLA Ops:
  7.2 65.4 %all-gather.11.cloned.1.call-start = ((), (), s32[]{:S(2)}) async-start(), calls=%async_computation.14 | async-start | bytes 2654208 | tf_op jit(solution)/shard_map/all_gather | solution.py:58
  20.0 73.0 %all-gather.9.cloned.1.call-start = ((), (), s32[]{:S(2)}) async-start(), calls=%async_computation.13 | async-start | bytes 1966080 | tf_op jit(solution)/shard_map/all_gather | solution.py:58
  22.1 124.4 %all-gather.13.cloned.1.call-start = ((), (), s32[]{:S(2)}) async-start(), calls=%async_computation.15 | async-start | bytes 2359296 | tf_op jit(solution)/shard_map/all_gather | solution.py:58
  98.7 11.9 all-to-all-start.1
  102.2 115.0 %all-gather.15.cloned.1.call-start = ((), (), s32[]{:S(2)}) async-start(), calls=%async_computation.16 | async-start | bytes 4423680 | tf_op jit(solution)/shard_map/all_gather | solution.py:58
  111.4 136.0 %reduce-scatter.11.cloned.1.call-start = ((), (), s32[]{:S(2)}) async-start(), calls=%async_computation.17 | async-start | bytes 1966080 | tf_op jit(solution)/shard_map/reduce_scatter | solution.py:62
  155.4 65.9 %copy-start.22 = (f32[128,1536]{1,0:T(8,128)S(1)}, f32[128,1536]{1,0:T(8,128)}, u32[]{:S(2)}) copy-start(f32[128,1536]{1,0:T(8,128)} %param.34) | copy-start | bytes 2359300
  156.3 92.4 %copy-start.47 = (bf16[3,512,128]{1,2,0:T(8,128)(2,1)}, bf16[3,512,128]{1,2,0:T(8,128)(2,1)S(1)}, u32[]{:S(2)}) copy-start(bf16[3,512,128]{1,2,0:T(8,128)(2,1)S(1)} %fusion.130) | copy-start | bytes 1179652
  156.4 91.1 %copy-start.8 = (f32[128,1536]{1,0:T(8,128)S(1)}, f32[128,1536]{1,0:T(8,128)}, u32[]{:S(2)}) copy-start(f32[128,1536]{1,0:T(8,128)} %param.33) | copy-start | bytes 2359300
  220.7 315.7 %reduce-scatter.15.cloned.1.call-start = ((), (), s32[]{:S(2)}) async-start(), calls=%async_computation.21 | async-start | bytes 15728640 | tf_op jit(solution)/shard_map/reduce_scatter | solution.py:62
  266.7 144.2 %slice-start = ((s8[6291456]{0:T(1024)(128)(4,1)}), s8[4194304]{0:T(1024)(128)(4,1)S(1)}, s32[]{:S(2)}) async-start(s8[6291456]{0:T(1024)(128)(4,1)} %bitcast.282), calls=%async_computation.27 | async-start | bytes 8388608
  437.5 187.2 %all-gather.21.cloned.1.call-start = ((), (), s32[]{:S(2)}) async-start(), calls=%async_computation.22 | async-start | bytes 15728640 | tf_op jit(solution)/shard_map/all_gather | solution.py:58
  542.4 109.9 %all-gather.17.cloned.1.call-start = ((), (), s32[]{:S(2)}) async-start(), calls=%async_computation.18 | async-start | bytes 1966080 | tf_op jit(solution)/shard_map/all_gather | solution.py:58
  646.8 144.7 %all-to-all-start.3 = ((bf16[32,8,16,768]{3,2,1,0:T(8,128)(2,1)}), bf16[32,8,16,768]{3,2,1,0:T(8,128)(2,1)}, u32[]{:S(2)}, u32[]{:S(2)}) async-start(bf16[32,8,16,768]{3,2,1,0:T(8,128)(2,1)} %copy.319), calls=%async_computation.6 | async-start | bytes 12582912 | tf_op jit(solution)/shard_map/all_to_all | solution.py:66
  651.6 50.9 %all-gather.19.cloned.1.call-start = ((), (), s32[]{:S(2)}) async-start(), calls=%async_computation.19 | async-start | bytes 1966080 | tf_op jit(solution)/shard_map/all_gather | solution.py:58
  652.3 108.5 %reduce-scatter.13.cloned.1.call-start = ((), (), s32[]{:S(2)}) async-start(), calls=%async_computation.20 | async-start | bytes 3932160 | tf_op jit(solution)/shard_map/reduce_scatter | solution.py:62
  709.1 165.7 %all-gather.23.cloned.1.call-start = ((), (), s32[]{:S(2)}) async-start(), calls=%async_computation.23 | async-start | bytes 2129920 | tf_op jit(solution)/shard_map/all_gather | solution.py:58
  895.5 71.8 %copy-start.4 = (f32[3,512,128]{2,1,0:T(8,128)S(1)}, f32[3,512,128]{2,1,0:T(8,128)}, u32[]{:S(2)}) copy-start(f32[3,512,128]{2,1,0:T(8,128)} %get-tuple-element.136) | copy-start | bytes 2359300
  895.5 120.1 %all-to-all-start.4 = ((bf16[8,512,256]{1,2,0:T(8,128)(2,1)}), bf16[8,512,256]{1,2,0:T(8,128)(2,1)S(1)}, u32[]{:S(2)}, u32[]{:S(2)}) async-start(bf16[8,512,256]{1,2,0:T(8,128)(2,1)} %copy.326), calls=%async_computation.7 | async-start | bytes 4194304 | tf_op jit(solution)/shard_map/all_to_all | solution.py:66
  967.0 130.3 %reduce-scatter.17.cloned.1.call-start = ((), (), s32[]{:S(2)}) async-start(), calls=%async_computation.24 | async-start | bytes 1966080 | tf_op jit(solution)/shard_map/reduce_scatter | solution.py:62
  1021.6 114.7 %reduce-scatter.21.cloned.1.call-start = ((), (), s32[]{:S(2)}) async-start(), calls=%async_computation.26 | async-start | bytes 4423680 | tf_op jit(solution)/shard_map/reduce_scatter | solution.py:62
  1034.3 174.5 %reduce-scatter.19.cloned.1.call-start = ((), (), s32[]{:S(2)}) async-start(), calls=%async_computation.25 | async-start | bytes 2654208 | tf_op jit(solution)/shard_map/reduce_scatter | solution.py:62
  1136.3 11.9 all-to-all-start.6
  1208.8 9.8 all-to-all-start.5
  (87 other events, 1347.8 us)
Sparse Core Ops, SparseCore 0:
  20.1 52.4 all-gather.10
  74.8 18.1 all-gather.8
  97.4 49.1 all-gather.12
  149.2 68.0 all-gather.14
  220.8 26.6 reduce-scatter.10
  437.6 98.7 reduce-scatter.14
  542.6 82.0 all-gather.20
  626.8 19.6 all-gather.16
  654.5 47.9 all-gather.18
  709.2 51.5 reduce-scatter.12
  853.2 21.4 all-gather.22
  1021.7 26.1 reduce-scatter.16
  1051.6 84.6 reduce-scatter.20
  1139.7 69.1 reduce-scatter.18
